TPU v7x, 512 devices: a whole 4x8x8 slice. The times are simulated.
512 devices in a mesh: dp: 16 (over z, core), tp: 32 (over y, x).
Axes of the slice: x: 4, y: 8, z: 8, core: 2. Of those that a mesh axis runs over, the one named last changes fastest.
Arguments:
- q_new: bfloat16 [512, 1536], P(('dp', 'tp'))
- new_key_value: bfloat16 [512, 512], P(('dp', 'tp')), may hold values from -6 to 6
- resid_dec: bfloat16 [512, 1536], P(('dp', 'tp')), may hold values from -6 to 6
- placing: int32 [512], replicated, may hold values from 0 to 511, as said below
- lengths: int32 [512], P('dp'), may hold values from 5 to 2048, as said below
- write_pos: int32 [512], P('dp'), may hold values from 4 to 2047, as said below
- k_cache: bfloat16 [512, 2, 2048, 128], P('dp', None, 'tp')
- value_cache: bfloat16 [512, 2, 2048, 128], P('dp', None, 'tp'), may hold values from -6 to 6
- w_out: bfloat16 [1536, 1536], P(None, 'tp'), may hold values from -0.15625 to 0.15625
- x_pre: bfloat16 [32256, 1536], P(('dp', 'tp')), may hold values from -6 to 6
- routes: int32 [32768, 4], P(('dp', 'tp')), may hold values from 0 to 31, all different within a row; in each aligned block of 64 rows (0 to 63, 64 to 127, ...) at most 16 rows name the same one
- route_scale: float32 [32768, 4], P(('dp', 'tp')), may hold values from 0.2 to 2
- moe_gain: float32 [1536], replicated, may hold values from 0.5 to 1.5
- w_gate: bfloat16 [32, 768, 1536], P('tp', 'dp'), may hold values from -0.15625 to 0.15625
- w_up: bfloat16 [32, 768, 1536], P('tp', 'dp'), may hold values from -0.15625 to 0.15625
- w_down: bfloat16 [32, 768, 1536], P('tp', 'dp'), may hold values from -0.21875 to 0.21875
Outputs:
- out_pre: bfloat16 [32256, 1536], P(('dp', 'tp'))
- out_dec: bfloat16 [512, 1536], P(('dp', 'tp'))
Inputs may be any that keep to these rules, and one draw needn't show every extreme that they name: Each of 0 to 511 appears once; cache row j belongs to request placing[j]. `lengths`: a cache row is either full (2048 live slots) or filled from slot 0 up; some row is full. `write_pos`: below the row's length; a row that is not full writes at its length - 1, a full row anywhere past the sink slots. `routes`: the 64 rows of one device name any one expert at most 16 times.
All inputs are finite; a program needn't handle non-finite values.
Results may differ from a plain program's by a relative error of at most 0.007.
Values may be sent and summed in bfloat16 or wider, within the bound.
No kernel may reach another device: no remote copies, remote signals or barrier semaphores. Data moves between devices by JAX's collectives and lax.ppermute only.
A program may use at most 64 MiB of HBM per device.

v0:
```python
import jax
import jax.numpy as jnp
from jax import lax
from jax.sharding import PartitionSpec as P

HIGHEST = lax.Precision.HIGHEST


def contract_rows(left_rows, unit_rows):
    return lax.dot_general(
        left_rows, unit_rows, (((1,), (1,)), ((), ())), preferred_element_type=jnp.float32
    )


def on_device(
    q_new,
    new_key_value,
    resid_dec,
    placing,
    lengths,
    write_pos,
    k_cache,
    value_cache,
    w_out,
    x_pre,
    routes,
    route_scale,
    moe_gain,
    w_gate,
    w_up,
    w_down,
):
    tp_size = lax.axis_size("tp")
    dp_group = lax.axis_index("dp")
    tp_lane = lax.axis_index("tp")
    group_reqs = k_cache.shape[0]
    kv_heads = k_cache.shape[1]
    slot_dev = k_cache.shape[2]
    head_size = k_cache.shape[3]
    query_width = q_new.shape[1]
    per_group = query_width // head_size // kv_heads
    fetched = (
        lax.all_gather(w_gate, "dp", axis=1, tiled=True),
        lax.all_gather(w_up, "dp", axis=1, tiled=True),
        lax.all_gather(w_down, "dp", axis=1, tiled=True),
    )
    all_query, all_new = (
        lax.all_gather(q_new, ("dp", "tp"), axis=0, tiled=True),
        lax.all_gather(new_key_value, ("dp", "tp"), axis=0, tiled=True),
    )
    my_rows = lax.dynamic_slice_in_dim(placing, dp_group * group_reqs, group_reqs)
    query_rows = jnp.take(all_query, my_rows, axis=0)
    fresh_rows = jnp.take(all_new, my_rows, axis=0)
    slot_ids = tp_lane * slot_dev + jnp.arange(slot_dev, dtype=jnp.int32)
    incoming_key = fresh_rows[:, : kv_heads * head_size].reshape(group_reqs, kv_heads, 1, head_size)
    incoming_value = fresh_rows[:, kv_heads * head_size :].reshape(
        group_reqs, kv_heads, 1, head_size
    )
    written = (slot_ids[None, :] == write_pos[:, None])[:, None, :, None]
    key_rows = jnp.where(written, incoming_key, k_cache)
    value_rows = jnp.where(written, incoming_value, value_cache).astype(jnp.float32)
    query_head_list = query_rows.reshape(group_reqs, kv_heads, per_group, head_size)
    scores = jnp.einsum(
        "rgqd,rgsd->rgqs", query_head_list, key_rows, preferred_element_type=jnp.float32
    ) * head_size ** (-0.5)
    is_valid = (slot_ids[None, :] < lengths[:, None])[:, None, None, :]
    masked = jnp.where(is_valid, scores, -1e30)
    local_peak = jnp.max(masked, axis=-1)
    peak = lax.pmax(local_peak, "tp")
    weights = jnp.where(is_valid, jnp.exp(masked - peak[..., None]), 0.0)
    local_total = jnp.sum(weights, axis=-1)
    local_mixed = jnp.einsum("rgqs,rgsd->rgqd", weights, value_rows, precision=HIGHEST)
    weight_total, mixed_sum = lax.psum((local_total, local_mixed), "tp")
    attention = (
        (mixed_sum / weight_total[..., None]).reshape(group_reqs, query_width).astype(jnp.bfloat16)
    )
    projected = jnp.dot(attention, w_out, preferred_element_type=jnp.float32).astype(jnp.bfloat16)
    cache_row = lax.all_to_all(projected, "tp", split_axis=0, concat_axis=1, tiled=True)
    all_proj = lax.all_gather(cache_row, ("dp", "tp"), axis=0, tiled=True)
    total_reqs = placing.shape[0]
    my_request = dp_group * tp_size + tp_lane
    where_cached = jnp.sum(
        jnp.where(placing == my_request, jnp.arange(total_reqs, dtype=jnp.int32), 0)
    )
    proj_home = lax.dynamic_slice_in_dim(all_proj, where_cached, 1, 0)
    hidden_dec = (resid_dec.astype(jnp.float32) + proj_home.astype(jnp.float32)).astype(
        jnp.bfloat16
    )
    moe_rows = jnp.concatenate([x_pre, hidden_dec], axis=0)
    rows_dev = moe_rows.shape[0]
    width = moe_rows.shape[1]
    top_count = routes.shape[1]
    experts = tp_size * w_gate.shape[0]
    capacity = min(2 * rows_dev * top_count // experts, rows_dev)
    rows_f32 = moe_rows.astype(jnp.float32)
    mean_square = jnp.mean(rows_f32 * rows_f32, axis=-1, keepdims=True)
    normed = (rows_f32 * lax.rsqrt(mean_square + 1e-06) * moe_gain).astype(jnp.bfloat16)
    route_weight = route_scale / jnp.sum(route_scale, axis=-1, keepdims=True)
    expert_ids = routes.reshape(rows_dev * top_count)
    onehot = (expert_ids[:, None] == jnp.arange(experts, dtype=jnp.int32)[None, :]).astype(
        jnp.int32
    )
    position = jnp.sum(onehot * (jnp.cumsum(onehot, axis=0) - onehot), axis=-1)
    slot_index = expert_ids * capacity + position
    slot_rows = slot_index.reshape(rows_dev, top_count)
    pick_table = jnp.any(
        slot_rows[:, :, None] == jnp.arange(experts * capacity, dtype=jnp.int32)[None, None, :],
        axis=1,
    ).astype(jnp.bfloat16)
    outgoing = jnp.einsum(
        "rc,rd->cd", pick_table, normed, preferred_element_type=jnp.float32
    ).astype(jnp.bfloat16)
    outgoing = outgoing.reshape(experts, capacity, width)
    received = lax.all_to_all(outgoing, "tp", split_axis=0, concat_axis=0, tiled=True)
    flat_rows = received.reshape(-1, received.shape[-1])
    gate = contract_rows(flat_rows, fetched[0][0])
    upper = contract_rows(flat_rows, fetched[1][0])
    active = (jnp.maximum(gate, 0.0) * upper).astype(jnp.bfloat16)
    output = jnp.dot(active, fetched[2][0], preferred_element_type=jnp.float32)
    expert_out = output.astype(jnp.bfloat16).reshape(received.shape)
    returned = lax.all_to_all(expert_out, "tp", split_axis=0, concat_axis=0, tiled=True)
    flat_back = returned.reshape(experts * capacity, width)
    picked = jnp.take(flat_back, slot_index, axis=0).reshape(rows_dev, top_count, width)
    mixture = jnp.sum(route_weight[:, :, None] * picked.astype(jnp.float32), axis=1)
    moe_out = (rows_f32 + mixture).astype(jnp.bfloat16)
    return (moe_out[: rows_dev - 1], moe_out[rows_dev - 1 :])


def solution(mesh):
    placed = (
        P(("dp", "tp"), None),
        P(("dp", "tp"), None),
        P(("dp", "tp"), None),
        P(),
        P("dp"),
        P("dp"),
        P("dp", None, "tp", None),
        P("dp", None, "tp", None),
        P(None, "tp"),
        P(("dp", "tp"), None),
        P(("dp", "tp"), None),
        P(("dp", "tp"), None),
        P(),
        P("tp", "dp", None),
        P("tp", "dp", None),
        P("tp", "dp", None),
    )
    return jax.shard_map(
        on_device,
        mesh=mesh,
        in_specs=placed,
        out_specs=(P(("dp", "tp"), None), P(("dp", "tp"), None)),
        check_vma=False,
    )
```

profile of v0, /device:TPU:4, one launch (start us, length us, event | category | flops | bytes accessed | tf_op | source)
XLA Modules:
  0.0 762.3 jit_solution(4975138523507420202)
XLA Ops:
  7.2 0.7 all-gather.15.cloned.1.call-update
  8.0 132.2 %all-gather.1 = bf16[512,1,512]{2,1,0:T(2,128)(2,1)S(1)} all-gather(bf16[1,1,512]{2,1,0:T(2,128)(2,1)} %bitcast.66), channel_id=1, replica_groups=mesh['dp'=16,'tp'=32] {'dp','tp'}, dimensions={0}, use_global_device_ids=true | all-gather | bytes 525312 | tf_op jit(solution)/shard_map/all_gather | solution.py:49
  140.4 0.6 gather_fusion.1
  141.3 2.3 copy.59
  143.6 0.6 gather_fusion
  144.4 1.1 fusion.45
  145.6 138.1 %pmax.7 = f32[32,2,6]{2,1,0:T(2,128)S(1)} all-reduce(f32[32,2,6]{2,1,0:T(2,128)S(1)} %get-tuple-element.10), channel_id=1, replica_groups=mesh['dp'=16,'tp'=32] {'tp'}, use_global_device_ids=true, to_apply=%region_1.2 | all-reduce | flops 384 | bytes 3072 | tf_op jit(solution)/shard_map/pmax | solution.py:69
  283.7 1.9 fusion.9
  286.0 137.7 %psum.15 = f32[32,2,6]{2,1,0:T(2,128)S(1)} all-reduce(f32[32,2,6]{2,1,0:T(2,128)S(1)} %fusion.23), channel_id=1, replica_groups=mesh['dp'=16,'tp'=32] {'tp'}, use_global_device_ids=true, to_apply=%region_4.5 | all-reduce | flops 384 | bytes 3072 | tf_op jit(solution)/shard_map/psum | solution.py:73
  423.7 13.1 %all-reduce.2.cloned.1.call-done = f32[32,2,6,128]{3,2,1,0:T(8,128)} async-done(((f32[32,2,6,128]{3,2,1,0:T(8,128)}), f32[32,2,6,128]{3,2,1,0:T(8,128)}) %all-reduce.2.cloned.1.call-update) | async-done | bytes 196624 | tf_op jit(solution)/shard_map/psum | solution.py:73
  436.8 1.1 divide_convert_fusion
  438.2 14.8 %all_to_all.26 = bf16[32,1,48]{2,1,0:T(2,128)(2,1)S(1)} all-to-all(bf16[32,1,48]{2,1,0:T(2,128)(2,1)S(1)} %copy.45), channel_id=1, replica_groups=mesh['dp'=16,'tp'=32] {'tp'}, dimensions={0} | all-to-all | bytes 6144 | tf_op jit(solution)/shard_map/all_to_all | solution.py:78
  453.1 0.7 reshape.210
  453.8 0.5 all-gather.11.cloned.1.call-update
  454.4 0.5 all-gather.13.cloned.1.call-update
  455.9 0.6 reduce-window.6
  457.1 0.6 select_reduce_fusion
  459.7 107.4 %all-gather.17.cloned.1.call-done = bf16[512,1,1536]{2,1,0:T(2,128)(2,1)} async-done(((bf16[1,1,1536]{2,1,0:T(2,128)(2,1)}), bf16[512,1,1536]{2,1,0:T(2,128)(2,1)}) %all-gather.17.cloned.1.call-update) | async-done | bytes 1572880 | tf_op jit(solution)/shard_map/all_gather | solution.py:79
  567.1 0.7 fusion.37
  568.0 1.8 convolution_convert_fusion.1
  569.8 7.1 all-to-all-start.1
  576.9 31.7 %all-gather.11.cloned.1.call-done = bf16[1,768,1536]{2,1,0:T(8,128)(2,1)} async-done(((bf16[1,48,1536]{2,1,0:T(8,128)(2,1)}), bf16[1,768,1536]{2,1,0:T(8,128)(2,1)}) %all-gather.11.cloned.1.call-update) | async-done | bytes 2359312 | tf_op jit(solution)/shard_map/all_gather | solution.py:44
  608.6 8.0 %all-to-all-done.1 = bf16[32,16,1536]{2,1,0:T(8,128)(2,1)S(1)} async-done(((bf16[32,16,1536]{2,1,0:T(8,128)(2,1)}), bf16[32,16,1536]{2,1,0:T(8,128)(2,1)S(1)}, u32[]{:S(2)}, u32[]{:S(2)}) %all-to-all-start.1) | async-done | bytes 1572896 | tf_op jit(solution)/shard_map/all_to_all | solution.py:114
  616.6 3.1 fusion.1
  619.7 32.1 %all-gather.13.cloned.1.call-done = bf16[1,768,1536]{2,1,0:T(8,128)(2,1)} async-done(((bf16[1,48,1536]{2,1,0:T(8,128)(2,1)}), bf16[1,768,1536]{2,1,0:T(8,128)(2,1)}) %all-gather.13.cloned.1.call-update) | async-done | bytes 2359312 | tf_op jit(solution)/shard_map/all_gather | solution.py:45
  651.9 43.5 %all-gather.9.cloned.1.call-done = bf16[1,768,1536]{2,1,0:T(8,128)(2,1)} async-done(((bf16[1,48,1536]{2,1,0:T(8,128)(2,1)}), bf16[1,768,1536]{2,1,0:T(8,128)(2,1)}) %all-gather.9.cloned.1.call-update) | async-done | bytes 2359312 | tf_op jit(solution)/shard_map/all_gather | solution.py:43
  695.4 6.7 convolution_convert_fusion
  702.1 10.0 %all-to-all-start.2 = ((bf16[32,16,1536]{2,1,0:T(8,128)(2,1)}), bf16[32,16,1536]{2,1,0:T(8,128)(2,1)S(1)}, u32[]{:S(2)}, u32[]{:S(2)}) async-start(bf16[32,16,1536]{2,1,0:T(8,128)(2,1)} %bitcast.10), calls=%async_computation.2 | async-start | bytes 3145728 | tf_op jit(solution)/shard_map/all_to_all | solution.py:121
  712.6 39.2 %all-to-all-done.2 = bf16[32,16,1536]{2,1,0:T(8,128)(2,1)S(1)} async-done(((bf16[32,16,1536]{2,1,0:T(8,128)(2,1)}), bf16[32,16,1536]{2,1,0:T(8,128)(2,1)S(1)}, u32[]{:S(2)}, u32[]{:S(2)}) %all-to-all-start.2) | async-done | bytes 1572896 | tf_op jit(solution)/shard_map/all_to_all | solution.py:121
  751.8 1.3 gather_fusion.2
  753.2 1.5 multiply_reduce_fusion
  754.8 0.7 slice.34
  (74 shorter events, 3.9 us)
Async XLA Ops:
  7.2 430.9 %copy-start = (bf16[1536,48]{0,1:T(8,128)(2,1)S(1)}, bf16[1536,48]{0,1:T(8,128)(2,1)}, u32[]{:S(2)}) copy-start(bf16[1536,48]{0,1:T(8,128)(2,1)} %param.24) | copy-start | bytes 442372
  7.2 133.2 %copy-start.7 = (s32[512]{0:T(512)S(1)}, s32[512]{0:T(512)}, u32[]{:S(2)}) copy-start(s32[512]{0:T(512)} %param.19) | copy-start | bytes 6148
  7.2 134.1 %all-gather.15.cloned.1.call-start = ((), (), s32[]{:S(2)}) async-start(), calls=%async_computation.7 | async-start | bytes 3151872 | tf_op jit(solution)/shard_map/all_gather | solution.py:48
  7.9 428.9 %all-reduce.2.cloned.1.call-start = ((), (), s32[]{:S(2)}) async-start(), calls=%async_computation.3 | async-start | bytes 524288 | tf_op jit(solution)/shard_map/psum | solution.py:73
  8.0 133.2 %copy-start.8 = (s32[32]{0:T(128)S(1)}, s32[32]{0:T(128)}, u32[]{:S(2)}) copy-start(s32[32]{0:T(128)} %param.20) | copy-start | bytes 388
  8.0 133.2 %copy-start.9 = (s32[32]{0:T(128)S(1)}, s32[32]{0:T(128)}, u32[]{:S(2)}) copy-start(s32[32]{0:T(128)} %param.21) | copy-start | bytes 388
  141.3 3.1 copy-start.10
  144.3 139.4 %copy-start.11 = (bf16[32,2,64,128]{3,2,1,0:T(8,128)(2,1)S(1)}, bf16[32,2,64,128]{3,2,1,0:T(8,128)(2,1)}, u32[]{:S(2)}) copy-start(bf16[32,2,64,128]{3,2,1,0:T(8,128)(2,1)} %param.23) | copy-start | bytes 3145732
  285.6 169.9 %copy-start.3 = (s32[64,4]{0,1:T(4,128)S(1)}, s32[64,4]{0,1:T(4,128)}, u32[]{:S(2)}) copy-start(s32[64,4]{0,1:T(4,128)} %param.26) | copy-start | bytes 3076
  285.6 281.5 %copy-start.6 = (bf16[1,1536]{1,0:T(2,128)(2,1)S(1)}, bf16[1,1536]{1,0:T(2,128)(2,1)}, u32[]{:S(2)}) copy-start(bf16[1,1536]{1,0:T(2,128)(2,1)} %param.18) | copy-start | bytes 9220
  285.6 282.2 %copy-start.1 = (bf16[63,1536]{1,0:T(8,128)(2,1)S(1)}, bf16[63,1536]{1,0:T(8,128)(2,1)}, u32[]{:S(2)}) copy-start(bf16[63,1536]{1,0:T(8,128)(2,1)} %param.25) | copy-start | bytes 580612
  285.6 282.4 %copy-start.4 = (f32[1536]{0:T(1024)S(1)}, f32[1536]{0:T(1024)}, u32[]{:S(2)}) copy-start(f32[1536]{0:T(1024)} %param.28) | copy-start | bytes 18436
  285.6 281.5 %all-gather.17.cloned.1.call-start = ((), (), s32[]{:S(2)}) async-start(), calls=%async_computation.8 | async-start | bytes 3151872 | tf_op jit(solution)/shard_map/all_gather | solution.py:79
  453.8 154.9 %all-gather.11.cloned.1.call-start = ((), (), s32[]{:S(2)}) async-start(), calls=%async_computation.5 | async-start | bytes 2506752 | tf_op jit(solution)/shard_map/all_gather | solution.py:44
  454.4 197.5 %all-gather.13.cloned.1.call-start = ((), (), s32[]{:S(2)}) async-start(), calls=%async_computation.6 | async-start | bytes 2506752 | tf_op jit(solution)/shard_map/all_gather | solution.py:45
  454.9 240.4 %all-gather.9.cloned.1.call-start = ((), (), s32[]{:S(2)}) async-start(), calls=%async_computation.4 | async-start | bytes 2506752 | tf_op jit(solution)/shard_map/all_gather | solution.py:43
  569.8 46.8 %all-to-all-start.1 = ((bf16[32,16,1536]{2,1,0:T(8,128)(2,1)}), bf16[32,16,1536]{2,1,0:T(8,128)(2,1)S(1)}, u32[]{:S(2)}, u32[]{:S(2)}) async-start(bf16[32,16,1536]{2,1,0:T(8,128)(2,1)} %bitcast.5), calls=%async_computation.1 | async-start | bytes 3145728 | tf_op jit(solution)/shard_map/all_to_all | solution.py:114
  702.1 10.3 %copy-start.5 = (f32[64,4]{0,1:T(4,128)S(1)}, f32[64,4]{0,1:T(4,128)}, u32[]{:S(2)}) copy-start(f32[64,4]{0,1:T(4,128)} %param.27) | copy-start | bytes 3076
  702.1 49.7 %all-to-all-start.2 = ((bf16[32,16,1536]{2,1,0:T(8,128)(2,1)}), bf16[32,16,1536]{2,1,0:T(8,128)(2,1)S(1)}, u32[]{:S(2)}, u32[]{:S(2)}) async-start(bf16[32,16,1536]{2,1,0:T(8,128)(2,1)} %bitcast.10), calls=%async_computation.2 | async-start | bytes 3145728 | tf_op jit(solution)/shard_map/all_to_all | solution.py:121
  754.8 0.7 copy-start.2
Sparse Core Ops, SparseCore 0:
  12.2 121.8 all-gather.14
  285.8 150.9 all-reduce.1
  453.9 113.1 all-gather.16
  569.1 39.4 all-gather.10
  610.6 41.2 all-gather.12
  653.8 41.4 all-gather.8
where the time goes:
time: 763 us; the launch traced here: 762 us
  blocking collectives  423 us (55%)
  waiting for transfers between devices  277 us (36%)
  starting transfers between devices  17.3 us (2%)
  between operations  16.4 us (2%)
  matrix products  14.7 us (2%)
  local copies, waits for them, and re-layouts  7.97 us (1%)
    pmax x1, blocking collectives, on_device(): peak = lax.pmax(local_peak, 'tp')  138 us
    psum x1, blocking collectives, on_device(): weight_total, mixed_sum = lax.psum((local_total, local_mixed), 'tp')  138 us
    all_gather x1, blocking collectives, on_device(): lax.all_gather(new_key_value, ('dp', 'tp'), axis=0, tiled=True)  132 us
    all_gather x1, waiting for transfers between devices, on_device(): all_proj = lax.all_gather(cache_row, ('dp', 'tp'), axis=0, tiled=True)  107 us
    all_gather x1, waiting for transfers between devices, on_device(): lax.all_gather(w_gate, 'dp', axis=1, tiled=True)  43.5 us
    all_to_all x1, waiting for transfers between devices, on_device(): lax.all_to_all(expert_out, 'tp', split_axis=0, concat_axis=0, tiled=True)  39.2 us
    all_gather x1, waiting for transfers between devices, on_device(): lax.all_gather(w_down, 'dp', axis=1, tiled=True)  32.1 us
    all_gather x1, waiting for transfers between devices, on_device(): lax.all_gather(w_up, 'dp', axis=1, tiled=True)  31.7 us
  transfers between devices with their start and end apart: 8, of which 7 were waited for; matrix products, arithmetic and copies ran while one was open for 1% of the time, Pallas kernels for 0%

commit v1 on v0

--- a/solution.py
+++ b/solution.py
@@ -4,6 +4,19 @@
 from jax.sharding import PartitionSpec as P
 
 HIGHEST = lax.Precision.HIGHEST
+
+
+def ring_gather(x, axis, dim):
+    ways = lax.axis_size(axis)
+    up = [(d, (d + 1) % ways) for d in range(ways)]
+    down = [(d, (d - 1) % ways) for d in range(ways)]
+    earlier, later = ([x], [x])
+    for _ in range(ways // 2):
+        earlier.append(lax.ppermute(earlier[-1], axis, up))
+    for _ in range((ways - 1) // 2):
+        later.append(lax.ppermute(later[-1], axis, down))
+    line = jnp.concatenate([*earlier[::-1], *later[1:]], axis=dim)
+    return jnp.roll(line, (lax.axis_index(axis) - ways // 2) * x.shape[dim], axis=dim)
 
 
 def contract_rows(left_rows, unit_rows):
@@ -42,7 +55,7 @@
     fetched = (
         lax.all_gather(w_gate, "dp", axis=1, tiled=True),
         lax.all_gather(w_up, "dp", axis=1, tiled=True),
-        lax.all_gather(w_down, "dp", axis=1, tiled=True),
+        ring_gather(w_down, "dp", 1),
     )
     all_query, all_new = (
         lax.all_gather(q_new, ("dp", "tp"), axis=0, tiled=True),

time: 763 us -> 723 us (0.948)
  waiting for transfers between devices: 277 us -> 187 us
  local copies, waits for them, and re-layouts: 7.97 us -> 32.6 us
  starting transfers between devices: 17.3 us -> 38 us
    all_gather x1, waiting for transfers between devices: 107 us -> 53.7 us  [on_device(): all_proj = lax.all_gather(cache_row, ('dp', 'tp'), axis=0, tiled=True)]
    all_gather x1 -> x0, waiting for transfers between devices: 32.1 us -> none  [on_device(): lax.all_gather(w_down, 'dp', axis=1, tiled=True)]
    unnamed x28 -> x61, local copies, waits for them, and re-layouts: 3.28 us -> 26.4 us
    ppermute x0 -> x15, starting transfers between devices: none -> 20.9 us  [the longest x7 20.9 us: ring_gather(): later.append(lax.ppermute(later[-1], axis, down))]
    ppermute x0 -> x15, waiting for transfers between devices: none -> 20.6 us  [the longest x8 20.6 us: ring_gather(): earlier.append(lax.ppermute(earlier[-1], axis, up))]
    all_gather x1, waiting for transfers between devices: 43.5 us -> 30.9 us  [on_device(): lax.all_gather(w_gate, 'dp', axis=1, tiled=True)]
    all_gather x1, waiting for transfers between devices: 31.7 us -> 19.6 us  [on_device(): lax.all_gather(w_up, 'dp', axis=1, tiled=True)]
  transfers between devices with their start and end apart: 8 -> 22, of which waited for: 7 -> 14; matrix products, arithmetic and copies ran while one was open for 1% -> 5% of each run, Pallas kernels for 0% -> 0%
where the time goes in v1:
time: 723 us; the launch traced here: 722 us
  blocking collectives  423 us (59%)
  waiting for transfers between devices  187 us (26%)
  starting transfers between devices  38 us (5%)
  local copies, waits for them, and re-layouts  32.6 us (5%)
  matrix products  18.6 us (3%)
  between operations  16.1 us (2%)
  other arithmetic  7.54 us (1%)
    pmax x1, blocking collectives, on_device(): peak = lax.pmax(local_peak, 'tp')  138 us
    psum x1, blocking collectives, on_device(): weight_total, mixed_sum = lax.psum((local_total, local_mixed), 'tp')  138 us
    all_gather x1, blocking collectives, on_device(): lax.all_gather(new_key_value, ('dp', 'tp'), axis=0, tiled=True)  132 us
    all_gather x1, waiting for transfers between devices, on_device(): all_proj = lax.all_gather(cache_row, ('dp', 'tp'), axis=0, tiled=True)  53.7 us
    all_to_all x1, waiting for transfers between devices, on_device(): lax.all_to_all(expert_out, 'tp', split_axis=0, concat_axis=0, tiled=True)  39.2 us
    all_gather x1, waiting for transfers between devices, on_device(): lax.all_gather(w_gate, 'dp', axis=1, tiled=True)  30.9 us
    unnamed x61, local copies, waits for them, and re-layouts  26.4 us
    ppermute x7, starting transfers between devices, ring_gather(): later.append(lax.ppermute(later[-1], axis, down))  20.9 us
  transfers between devices with their start and end apart: 22, of which 14 were waited for; matrix products, arithmetic and copies ran while one was open for 5% of the time, Pallas kernels for 0%

profile of v1, /device:TPU:4, one launch (start us, length us, event | category | flops | bytes accessed | tf_op | source)
XLA Modules:
  0.0 722.2 jit_solution(16123469640966443627)
XLA Ops:
  8.0 132.2 %all-gather.1 = bf16[512,1,512]{2,1,0:T(2,128)(2,1)S(1)} all-gather(bf16[1,1,512]{2,1,0:T(2,128)(2,1)} %bitcast.66), channel_id=1, replica_groups=mesh['dp'=16,'tp'=32] {'dp','tp'}, dimensions={0}, use_global_device_ids=true | all-gather | bytes 525312 | tf_op jit(solution)/shard_map/all_gather | solution.py:62
  142.6 2.2 copy.59
  145.7 2.2 fusion.47
  147.8 138.1 %pmax.7 = f32[32,2,6]{2,1,0:T(2,128)S(1)} all-reduce(f32[32,2,6]{2,1,0:T(2,128)S(1)} %get-tuple-element.10), channel_id=1, replica_groups=mesh['dp'=16,'tp'=32] {'tp'}, use_global_device_ids=true, to_apply=%region_1.2 | all-reduce | flops 384 | bytes 3072 | tf_op jit(solution)/shard_map/pmax | solution.py:82
  286.0 3.0 fusion.10
  289.3 137.7 %psum.15 = f32[32,2,6]{2,1,0:T(2,128)S(1)} all-reduce(f32[32,2,6]{2,1,0:T(2,128)S(1)} %fusion.24), channel_id=1, replica_groups=mesh['dp'=16,'tp'=32] {'tp'}, use_global_device_ids=true, to_apply=%region_4.5 | all-reduce | flops 384 | bytes 3072 | tf_op jit(solution)/shard_map/psum | solution.py:86
  427.1 13.1 %all-reduce.2.cloned.1.call-done = f32[32,2,6,128]{3,2,1,0:T(8,128)} async-done(((f32[32,2,6,128]{3,2,1,0:T(8,128)}), f32[32,2,6,128]{3,2,1,0:T(8,128)}) %all-reduce.2.cloned.1.call-update) | async-done | bytes 196624 | tf_op jit(solution)/shard_map/psum | solution.py:86
  441.6 14.8 %all_to_all.26 = bf16[32,1,48]{2,1,0:T(2,128)(2,1)S(1)} all-to-all(bf16[32,1,48]{2,1,0:T(2,128)(2,1)S(1)} %copy.45), channel_id=1, replica_groups=mesh['dp'=16,'tp'=32] {'tp'}, dimensions={0} | all-to-all | bytes 6144 | tf_op jit(solution)/shard_map/all_to_all | solution.py:91
  457.8 5.8 collective-permute-done
  463.6 3.0 collective-permute-start.8
  466.5 2.8 collective-permute-done.1
  469.4 3.0 collective-permute-start.9
  472.3 2.8 collective-permute-done.2
  475.4 3.0 collective-permute-start.10
  478.4 2.6 collective-permute-done.3
  481.6 3.0 collective-permute-start.11
  484.6 2.2 collective-permute-done.4
  487.4 3.0 collective-permute-start.12
  490.4 2.2 collective-permute-done.5
  493.1 3.0 collective-permute-start.13
  496.1 2.2 collective-permute-done.6
  501.1 3.0 collective-permute-start.14
  516.8 53.7 %all-gather.14.cloned.1.call-done = bf16[512,1,1536]{2,1,0:T(2,128)(2,1)} async-done(((bf16[1,1,1536]{2,1,0:T(2,128)(2,1)}), bf16[512,1,1536]{2,1,0:T(2,128)(2,1)}) %all-gather.14.cloned.1.call-update) | async-done | bytes 1572880 | tf_op jit(solution)/shard_map/all_gather | solution.py:92
  571.4 1.8 convolution_convert_fusion.1
  573.2 7.1 all-to-all-start.1
  592.4 19.6 %all-gather.10.cloned.1.call-done = bf16[1,768,1536]{2,1,0:T(8,128)(2,1)} async-done(((bf16[1,48,1536]{2,1,0:T(8,128)(2,1)}), bf16[1,768,1536]{2,1,0:T(8,128)(2,1)}) %all-gather.10.cloned.1.call-update) | async-done | bytes 2359312 | tf_op jit(solution)/shard_map/all_gather | solution.py:57
  612.0 8.0 %all-to-all-done.1 = bf16[32,16,1536]{2,1,0:T(8,128)(2,1)S(1)} async-done(((bf16[32,16,1536]{2,1,0:T(8,128)(2,1)}), bf16[32,16,1536]{2,1,0:T(8,128)(2,1)S(1)}, u32[]{:S(2)}, u32[]{:S(2)}) %all-to-all-start.1) | async-done | bytes 1572896 | tf_op jit(solution)/shard_map/all_to_all | solution.py:127
  620.0 4.3 fusion.1
  624.3 30.9 %all-gather.8.cloned.1.call-done = bf16[1,768,1536]{2,1,0:T(8,128)(2,1)} async-done(((bf16[1,48,1536]{2,1,0:T(8,128)(2,1)}), bf16[1,768,1536]{2,1,0:T(8,128)(2,1)}) %all-gather.8.cloned.1.call-update) | async-done | bytes 2359312 | tf_op jit(solution)/shard_map/all_gather | solution.py:56
  655.2 7.2 convolution_convert_fusion
  662.4 9.9 %all-to-all-start.2 = ((bf16[32,16,1536]{2,1,0:T(8,128)(2,1)}), bf16[32,16,1536]{2,1,0:T(8,128)(2,1)S(1)}, u32[]{:S(2)}, u32[]{:S(2)}) async-start(bf16[32,16,1536]{2,1,0:T(8,128)(2,1)} %bitcast.10), calls=%async_computation.2 | async-start | bytes 3145728 | tf_op jit(solution)/shard_map/all_to_all | solution.py:134
  672.8 39.2 %all-to-all-done.2 = bf16[32,16,1536]{2,1,0:T(8,128)(2,1)S(1)} async-done(((bf16[32,16,1536]{2,1,0:T(8,128)(2,1)}), bf16[32,16,1536]{2,1,0:T(8,128)(2,1)S(1)}, u32[]{:S(2)}, u32[]{:S(2)}) %all-to-all-start.2) | async-done | bytes 1572896 | tf_op jit(solution)/shard_map/all_to_all | solution.py:134
  (135 shorter events, 39.7 us)
Async XLA Ops:
  7.2 434.2 %copy-start = (bf16[1536,48]{0,1:T(8,128)(2,1)S(1)}, bf16[1536,48]{0,1:T(8,128)(2,1)}, u32[]{:S(2)}) copy-start(bf16[1536,48]{0,1:T(8,128)(2,1)} %param.24) | copy-start | bytes 442372
  7.2 135.5 %all-gather.12.cloned.1.call-start = ((), (), s32[]{:S(2)}) async-start(), calls=%async_computation.6 | async-start | bytes 3151872 | tf_op jit(solution)/shard_map/all_gather | solution.py:61
  7.9 432.3 %all-reduce.2.cloned.1.call-start = ((), (), s32[]{:S(2)}) async-start(), calls=%async_computation.3 | async-start | bytes 524288 | tf_op jit(solution)/shard_map/psum | solution.py:86
  144.9 312.9 %copy-start.2 = (bf16[1,48,1536]{2,1,0:T(8,128)(2,1)S(1)}, bf16[1,48,1536]{2,1,0:T(8,128)(2,1)}, u32[]{:S(2)}) copy-start(bf16[1,48,1536]{2,1,0:T(8,128)(2,1)} %param.31) | copy-start | bytes 442372
  144.9 330.3 %copy-start.7 = (s32[64,4]{0,1:T(4,128)S(1)}, s32[64,4]{0,1:T(4,128)}, u32[]{:S(2)}) copy-start(s32[64,4]{0,1:T(4,128)} %param.26) | copy-start | bytes 3076
  144.9 353.4 %copy-start.11 = (s32[512]{0:T(512)S(1)}, s32[512]{0:T(512)}, u32[]{:S(2)}) copy-start(s32[512]{0:T(512)} %param.19) | copy-start | bytes 6148
  286.0 284.6 %copy-start.10 = (bf16[1,1536]{1,0:T(2,128)(2,1)S(1)}, bf16[1,1536]{1,0:T(2,128)(2,1)}, u32[]{:S(2)}) copy-start(bf16[1,1536]{1,0:T(2,128)(2,1)} %param.18) | copy-start | bytes 9220
  286.0 285.3 %copy-start.1 = (bf16[63,1536]{1,0:T(8,128)(2,1)S(1)}, bf16[63,1536]{1,0:T(8,128)(2,1)}, u32[]{:S(2)}) copy-start(bf16[63,1536]{1,0:T(8,128)(2,1)} %param.25) | copy-start | bytes 580612
  286.0 285.4 %copy-start.8 = (f32[1536]{0:T(1024)S(1)}, f32[1536]{0:T(1024)}, u32[]{:S(2)}) copy-start(f32[1536]{0:T(1024)} %param.28) | copy-start | bytes 18436
  289.0 281.5 %all-gather.14.cloned.1.call-start = ((), (), s32[]{:S(2)}) async-start(), calls=%async_computation.7 | async-start | bytes 3151872 | tf_op jit(solution)/shard_map/all_gather | solution.py:92
  457.1 154.9 %all-gather.10.cloned.1.call-start = ((), (), s32[]{:S(2)}) async-start(), calls=%async_computation.5 | async-start | bytes 2506752 | tf_op jit(solution)/shard_map/all_gather | solution.py:57
  457.7 197.5 %all-gather.8.cloned.1.call-start = ((), (), s32[]{:S(2)}) async-start(), calls=%async_computation.4 | async-start | bytes 2506752 | tf_op jit(solution)/shard_map/all_gather | solution.py:56
  457.8 5.8 collective-permute-start
  463.6 5.8 collective-permute-start.1
  463.6 5.8 collective-permute-start.8
  469.4 5.8 collective-permute-start.2
  469.4 6.0 collective-permute-start.9
  475.2 5.8 collective-permute-start.3
  475.4 6.1 collective-permute-start.10
  480.9 5.8 collective-permute-start.4
  481.6 5.8 collective-permute-start.11
  486.7 5.8 collective-permute-start.5
  487.4 5.7 collective-permute-start.12
  492.5 80.7 %copy-start.3 = (bf16[1,48,1536]{2,1,0:T(8,128)(2,1)}, bf16[1,48,1536]{2,1,0:T(8,128)(2,1)S(1)}, u32[]{:S(2)}) copy-start(bf16[1,48,1536]{2,1,0:T(8,128)(2,1)S(1)} %collective-permute-done.5) | copy-start | bytes 442372
  492.5 5.8 collective-permute-start.6
  493.1 8.0 %collective-permute-start.13 = (bf16[1,48,1536]{2,1,0:T(8,128)(2,1)S(1)}, bf16[1,48,1536]{2,1,0:T(8,128)(2,1)S(1)}, u32[]{:S(2)}, u32[]{:S(2)}) collective-permute-start(bf16[1,48,1536]{2,1,0:T(8,128)(2,1)S(1)} %collective-permute-done.12), channel_id=1, source_target_pairs={{0,480},{32,0},{64,32},{96,64},{128,96},{160,128},{192,160},{224,1... | collective-permute-start | bytes 442376 | tf_op jit(solution)/shard_map/ppermute | solution.py:17
  498.3 5.8 collective-permute-start.7
  501.1 72.2 %copy-start.4 = (bf16[1,48,1536]{2,1,0:T(8,128)(2,1)}, bf16[1,48,1536]{2,1,0:T(8,128)(2,1)S(1)}, u32[]{:S(2)}) copy-start(bf16[1,48,1536]{2,1,0:T(8,128)(2,1)S(1)} %collective-permute-done.13) | copy-start | bytes 442372
  501.1 13.1 %collective-permute-start.14 = (bf16[1,48,1536]{2,1,0:T(8,128)(2,1)S(1)}, bf16[1,48,1536]{2,1,0:T(8,128)(2,1)S(1)}, u32[]{:S(2)}, u32[]{:S(2)}) collective-permute-start(bf16[1,48,1536]{2,1,0:T(8,128)(2,1)S(1)} %collective-permute-done.13), channel_id=1, source_target_pairs={{0,480},{32,0},{64,32},{96,64},{128,96},{160,128},{192,160},{224,1... | collective-permute-start | bytes 442376 | tf_op jit(solution)/shard_map/ppermute | solution.py:17
  573.2 46.8 %all-to-all-start.1 = ((bf16[32,16,1536]{2,1,0:T(8,128)(2,1)}), bf16[32,16,1536]{2,1,0:T(8,128)(2,1)S(1)}, u32[]{:S(2)}, u32[]{:S(2)}) async-start(bf16[32,16,1536]{2,1,0:T(8,128)(2,1)} %bitcast.5), calls=%async_computation.1 | async-start | bytes 3145728 | tf_op jit(solution)/shard_map/all_to_all | solution.py:127
  624.3 48.3 %copy-start.9 = (f32[64,4]{0,1:T(4,128)S(1)}, f32[64,4]{0,1:T(4,128)}, u32[]{:S(2)}) copy-start(f32[64,4]{0,1:T(4,128)} %param.27) | copy-start | bytes 3076
  662.4 49.6 %all-to-all-start.2 = ((bf16[32,16,1536]{2,1,0:T(8,128)(2,1)}), bf16[32,16,1536]{2,1,0:T(8,128)(2,1)S(1)}, u32[]{:S(2)}, u32[]{:S(2)}) async-start(bf16[32,16,1536]{2,1,0:T(8,128)(2,1)} %bitcast.10), calls=%async_computation.2 | async-start | bytes 3145728 | tf_op jit(solution)/shard_map/all_to_all | solution.py:134
  (3 other events, 49.5 us)
Sparse Core Ops, SparseCore 0:
  12.2 121.8 all-gather.11
  289.1 150.9 all-reduce.1
  457.3 113.2 all-gather.13
  572.5 39.4 all-gather.9
  614.0 41.2 all-gather.7
